TPU v7x, 32 devices: a whole 2x2x4 slice. The times are simulated.
32 devices in a mesh: seq: 8 (over y, x, core), ch: 4 (over z).
Axes of the slice: x: 2, y: 2, z: 4, core: 2. Of those that a mesh axis runs over, the one named last changes fastest.
Arguments:
- out_gate: bfloat16 [4096, 1024], P('ch', 'seq'), may hold values from -6 to 6
- key_proj: bfloat16 [4096, 1024], P('ch', 'seq'), may hold values from -6 to 6
- value_proj: bfloat16 [4096, 1024], P('ch', 'seq'), may hold values from -6 to 6
- long_filter: bfloat16 [4096, 1024], P('ch', 'seq'), may hold values from -0.1875 to 0.1875
- skip_gain: float32 [4096], P('ch'), may hold values from -4 to 4
- residual: bfloat16 [4096, 1024], P('ch', 'seq'), may hold values from -6 to 6
- norm_gain: float32 [4096], P('ch'), may hold values from 0.5 to 1.5
Outputs:
- mixed: bfloat16 [4096, 1024], P('ch', 'seq')
- normed: bfloat16 [4096, 1024], P('ch', 'seq')
All inputs are finite; a program needn't handle non-finite values.
Results may differ from a plain program's by a relative error of at most 0.0075.
Values may be sent and summed in bfloat16 or wider, within the bound.
A program may use at most 64 MiB of HBM per device.

v0:
```python
import math
import jax
import jax.numpy as jnp
from jax import lax
from jax.sharding import PartitionSpec as P

D = 4096
HIGHEST = lax.Precision.HIGHEST


def tables(count, span, period):
    row_ids = jnp.arange(count, dtype=jnp.int32)[:, None]
    col_ids = jnp.arange(span, dtype=jnp.int32)[None, :]
    phases = (row_ids * col_ids % period).astype(jnp.float32) * (2.0 * math.pi / period)
    return (jnp.cos(phases), jnp.sin(phases))


def product(left, right):
    return jnp.dot(left, right, precision=HIGHEST, preferred_element_type=jnp.float32)


def block_spectrum(signal):
    width = signal.shape[1]
    cosine, sine = tables(width, 2 * width, 2 * width)
    return (product(signal, cosine), -product(signal, sine))


def block_inverse(real_part, imag_part):
    span = real_part.shape[1]
    cosine, sine = tables(span, span, span)
    return (product(real_part, cosine) - product(imag_part, sine)) / span


def index_convolve(input_real, input_imag, filter_real, filter_imag):
    blocks = input_real.shape[0]
    forward_cos, forward_sin = tables(2 * blocks, blocks, 2 * blocks)

    def forward(real_part, imag_part):
        return (
            product(forward_cos, real_part) + product(forward_sin, imag_part),
            product(forward_cos, imag_part) - product(forward_sin, real_part),
        )

    signal_real, signal_imag = forward(input_real, input_imag)
    kernel_real, kernel_imag = forward(filter_real, filter_imag)
    joint_real = signal_real * kernel_real - signal_imag * kernel_imag
    joint_imag = signal_real * kernel_imag + signal_imag * kernel_real
    back_cos, back_sin = tables(blocks, 2 * blocks, 2 * blocks)
    result_real = (product(back_cos, joint_real) - product(back_sin, joint_imag)) / (2 * blocks)
    result_imag = (product(back_cos, joint_imag) + product(back_sin, joint_real)) / (2 * blocks)
    return (result_real, result_imag)


def on_device(out_gate, key_proj, value_proj, long_filter, skip_gain, residual, norm_gain):
    chans, width = key_proj.shape
    blocks = lax.axis_size("seq")
    product_in = (key_proj.astype(jnp.float32) * value_proj.astype(jnp.float32)).astype(
        jnp.bfloat16
    )
    signal_f = product_in.astype(jnp.float32)
    whole_in, whole_filter = (
        lax.all_to_all(product_in, "seq", split_axis=0, concat_axis=1, tiled=True),
        lax.all_to_all(long_filter, "seq", split_axis=0, concat_axis=1, tiled=True),
    )
    group = whole_in.shape[0]

    def by_block(array):
        return (
            array.astype(jnp.float32)
            .reshape(group, blocks, width)
            .transpose(1, 0, 2)
            .reshape(blocks * group, width)
        )

    signal_real, signal_imag = block_spectrum(by_block(whole_in))
    kernel_real, kernel_imag = block_spectrum(by_block(whole_filter))
    result_real, result_imag = index_convolve(
        signal_real.reshape(blocks, -1),
        signal_imag.reshape(blocks, -1),
        kernel_real.reshape(blocks, -1),
        kernel_imag.reshape(blocks, -1),
    )
    timeline = block_inverse(
        result_real.reshape(blocks * group, 2 * width),
        result_imag.reshape(blocks * group, 2 * width),
    ).reshape(blocks, group, 2 * width)
    upper = timeline[:, :, width:]
    carried = jnp.concatenate([jnp.zeros((1, group, width), jnp.float32), upper[:-1]], axis=0)
    whole_out = (timeline[:, :, :width] + carried).transpose(1, 0, 2).reshape(group, blocks * width)
    convolved = lax.all_to_all(whole_out, "seq", split_axis=1, concat_axis=0, tiled=True)
    total = residual.astype(jnp.float32) + out_gate.astype(jnp.float32) * (
        convolved + skip_gain[:, None] * signal_f
    )
    squares = lax.psum(jnp.sum(total * total, axis=0), "ch")
    normed = total * lax.rsqrt(squares / D + 1e-06)[None, :] * norm_gain[:, None]
    return (total.astype(jnp.bfloat16), normed.astype(jnp.bfloat16))


def solution(mesh):
    return jax.shard_map(
        on_device,
        mesh=mesh,
        in_specs=(
            P("ch", "seq"),
            P("ch", "seq"),
            P("ch", "seq"),
            P("ch", "seq"),
            P("ch"),
            P("ch", "seq"),
            P("ch"),
        ),
        out_specs=(P("ch", "seq"), P("ch", "seq")),
        check_vma=False,
    )
```

profile of v0, /device:TPU:0, one launch (start us, length us, event | category | flops | bytes accessed | tf_op | source)
XLA Modules:
  0.0 86.7 jit_solution(10550059197464009538)
XLA Ops:
  1.7 11.9 %all_to_all.42 = bf16[8,128,128]{2,1,0:T(8,128)(2,1)S(1)} all-to-all(bf16[8,128,128]{2,1,0:T(8,128)(2,1)S(1)} %bitcast.44), channel_id=1, replica_groups=mesh['seq'=8,'ch'=4] {'seq'}, dimensions={0} | all-to-all | bytes 524288 | tf_op jit(solution)/shard_map/all_to_all | solution.py:62
  13.6 3.4 %all-to-all-start.1 = ((bf16[8,128,128]{2,1,0:T(8,128)(2,1)}), bf16[8,128,128]{2,1,0:T(8,128)(2,1)S(1)}, u32[]{:S(2)}, u32[]{:S(2)}) async-start(bf16[8,128,128]{2,1,0:T(8,128)(2,1)} %bitcast.45), calls=%async_computation.1 | async-start | bytes 524288 | tf_op jit(solution)/shard_map/all_to_all | solution.py:63
  19.2 4.7 %all-to-all-done.1 = bf16[8,128,128]{2,1,0:T(8,128)(2,1)S(1)} async-done(((bf16[8,128,128]{2,1,0:T(8,128)(2,1)}), bf16[8,128,128]{2,1,0:T(8,128)(2,1)S(1)}, u32[]{:S(2)}, u32[]{:S(2)}) %all-to-all-start.1) | async-done | bytes 262176 | tf_op jit(solution)/shard_map/all_to_all | solution.py:63
  23.9 2.1 %fusion.2 = f32[1024,256]{0,1:T(8,128)} fusion(bf16[1024,128]{1,0:T(8,128)(2,1)S(1)} %bitcast.40), kind=kOutput, calls=%fused_computation.11 | convolution fusion | flops 403374080 | bytes 1310720 | tf_op jit(solution)/shard_map/dot_general | solution.py:19
  26.0 2.1 %convolution_bitcast_fusion = f32[1024,256]{0,1:T(8,128)} fusion(bf16[1024,128]{1,0:T(8,128)(2,1)S(1)} %bitcast.41), kind=kOutput, calls=%fused_computation.12 | convolution fusion | flops 403111936 | bytes 1310720 | tf_op jit(solution)/shard_map/dot_general | solution.py:19
  28.3 1.2 %reshape.50 = f32[8,32768]{1,0:T(8,128)} reshape(f32[1024,256]{1,0:T(8,128)S(1)} %fusion.27) | data formatting | bytes 2097152 | tf_op jit(solution)/shard_map/reshape | solution.py:78
  29.4 2.6 %copy.10 = f32[1024,256]{1,0:T(8,128)} copy(f32[1024,256]{0,1:T(8,128)} %fusion.2) | data formatting | bytes 2097152 | tf_op jit(solution)/shard_map/neg | solution.py:25
  32.1 1.4 %reshape.54 = f32[8,32768]{1,0:T(8,128)S(1)} reshape(f32[1024,256]{1,0:T(8,128)} %copy.10) | data formatting | bytes 2097152 | tf_op jit(solution)/shard_map/reshape | solution.py:81
  33.5 1.4 %copy.9 = f32[1024,256]{1,0:T(8,128)} copy(f32[1024,256]{0,1:T(8,128)S(1)} %copy-done.1) | data formatting | bytes 2097152 | tf_op jit(solution)/shard_map/dot_general | solution.py:19
  34.8 1.4 %reshape.53 = f32[8,32768]{1,0:T(8,128)S(1)} reshape(f32[1024,256]{1,0:T(8,128)} %copy.9) | data formatting | bytes 2097152 | tf_op jit(solution)/shard_map/reshape | solution.py:80
  36.3 1.8 %fusion.46 = f32[16,32768]{1,0:T(8,128)S(1)} fusion(f32[8,32768]{1,0:T(8,128)S(1)} %reshape.53), kind=kOutput, calls=%fused_computation.67 | convolution fusion | flops 50333440 | bytes 3145728 | tf_op jit(solution)/shard_map/dot_general | solution.py:19
  38.1 1.8 %fusion.42 = f32[16,32768]{1,0:T(8,128)S(1)} fusion(f32[8,32768]{1,0:T(8,128)S(1)} %reshape.54), kind=kOutput, calls=%fused_computation.65 | convolution fusion | flops 50333440 | bytes 3145728 | tf_op jit(solution)/shard_map/dot_general | solution.py:19
  39.9 1.9 %convolution_add_fusion = f32[16,32768]{1,0:T(8,128)S(1)} fusion(f32[16,32768]{1,0:T(8,128)S(1)} %fusion.46, f32[8,32768]{1,0:T(8,128)S(1)} %reshape.54), kind=kOutput, calls=%fused_computation.2 | convolution fusion | flops 50857728 | bytes 5242880 | tf_op jit(solution)/shard_map/dot_general | solution.py:19
  41.8 2.1 %convolution_subtract_fusion = f32[16,32768]{1,0:T(8,128)S(1)} fusion(f32[16,32768]{1,0:T(8,128)S(1)} %fusion.42, f32[8,32768]{1,0:T(8,128)S(1)} %reshape.53), kind=kOutput, calls=%fused_computation | convolution fusion | flops 50857728 | bytes 5242880 | tf_op jit(solution)/shard_map/dot_general | solution.py:19
  43.9 1.8 %fusion.48 = f32[16,32768]{1,0:T(8,128)S(1)} fusion(f32[8,32768]{1,0:T(8,128)S(1)} %copy-done), kind=kOutput, calls=%fused_computation.68 | convolution fusion | flops 50333440 | bytes 3145728 | tf_op jit(solution)/shard_map/dot_general | solution.py:19
  45.8 1.8 %fusion.44 = f32[16,32768]{1,0:T(8,128)S(1)} fusion(f32[8,32768]{1,0:T(8,128)S(1)} %reshape.51), kind=kOutput, calls=%fused_computation.66 | convolution fusion | flops 50333440 | bytes 3145728 | tf_op jit(solution)/shard_map/dot_general | solution.py:19
  47.6 1.9 %convolution_add_fusion.1 = f32[16,32768]{1,0:T(8,128)S(1)} fusion(f32[16,32768]{1,0:T(8,128)S(1)} %fusion.48, f32[8,32768]{1,0:T(8,128)S(1)} %reshape.51), kind=kOutput, calls=%fused_computation.3 | convolution fusion | flops 50857728 | bytes 5242880 | tf_op jit(solution)/shard_map/dot_general | solution.py:19
  49.5 2.4 %multiply_add_fusion = (f32[16,32768]{1,0:T(8,128)S(1)}, f32[16,32768]{1,0:T(8,128)S(1)}) fusion(f32[16,32768]{1,0:T(8,128)S(1)} %convolution_add_fusion, f32[16,32768]{1,0:T(8,128)S(1)} %convolution_add_fusion.1, f32[16,32768]{1,0:T(8,128)S(1)} %convolution_subtract_fusion, f32[16,32768]{1,0:T(8,128)S(1)} %fusion.44, f32[8,32768]{1,0:T(8,128)S(1)} %copy-done), kind=kOutput, calls=%fused_computation.8 | convolution fusion | flops 54003456 | bytes 13631488 | tf_op jit(solution)/shard_map/dot_general | solution.py:19
  54.2 1.1 %fusion = f32[8,32768]{1,0:T(8,128)S(1)} fusion(f32[8,32768]{1,0:T(8,128)S(1)} %fusion.59, f32[16,32768]{1,0:T(8,128)S(1)} %get-tuple-element.5), kind=kOutput, calls=%fused_computation.5 | convolution fusion | flops 50857728 | bytes 4194304 | tf_op jit(solution)/shard_map/dot_general | solution.py:19
  55.4 1.1 %fusion.1 = f32[8,32768]{1,0:T(8,128)S(1)} fusion(f32[8,32768]{1,0:T(8,128)S(1)} %fusion.61, f32[16,32768]{1,0:T(8,128)S(1)} %get-tuple-element.4), kind=kOutput, calls=%fused_computation.7 | convolution fusion | flops 50857728 | bytes 4194304 | tf_op jit(solution)/shard_map/dot_general | solution.py:19
  56.7 2.2 %fusion.11 = f32[1024,256]{1,0:T(8,128)S(1)} fusion(f32[1024,256]{1,0:T(8,128)S(1)} %reshape.55), kind=kOutput, calls=%fused_computation.31 | convolution fusion | flops 806223872 | bytes 2097152 | tf_op jit(solution)/shard_map/dot_general | solution.py:19
  59.1 2.0 %fusion.3 = f32[1024,256]{1,0:T(8,128)S(1)} fusion(f32[1024,256]{1,0:T(8,128)S(1)} %fusion.11, f32[1024,256]{1,0:T(8,128)S(1)} %reshape.56), kind=kOutput, calls=%fused_computation.15 | convolution fusion | flops 806748160 | bytes 3145728 | tf_op jit(solution)/shard_map/dot_general | solution.py:19
  61.2 12.3 %all_to_all.43 = f32[128,8,128]{2,0,1:T(8,128)S(1)} all-to-all(f32[128,8,128]{2,0,1:T(8,128)S(1)} %fusion.4), channel_id=1, replica_groups=mesh['seq'=8,'ch'=4] {'seq'}, dimensions={1} | all-to-all | bytes 1048576 | tf_op jit(solution)/shard_map/all_to_all | solution.py:90
  73.7 12.0 %psum.7 = f32[128]{0:T(128)S(1)} all-reduce(f32[128]{0:T(128)S(1)} %get-tuple-element.2), channel_id=1, replica_groups=mesh['seq'=8,'ch'=4] {'ch'}, use_global_device_ids=true, to_apply=%region_1.2 | all-reduce | flops 128 | bytes 1024 | tf_op jit(solution)/shard_map/psum | solution.py:94
  (25 shorter events, 7.4 us)
Async XLA Ops:
  13.6 10.3 %all-to-all-start.1 = ((bf16[8,128,128]{2,1,0:T(8,128)(2,1)}), bf16[8,128,128]{2,1,0:T(8,128)(2,1)S(1)}, u32[]{:S(2)}, u32[]{:S(2)}) async-start(bf16[8,128,128]{2,1,0:T(8,128)(2,1)} %bitcast.45), calls=%async_computation.1 | async-start | bytes 524288 | tf_op jit(solution)/shard_map/all_to_all | solution.py:63
  29.4 4.0 %copy-start.1 = (f32[1024,256]{0,1:T(8,128)S(1)}, f32[1024,256]{0,1:T(8,128)}, u32[]{:S(2)}) copy-start(f32[1024,256]{0,1:T(8,128)} %convolution_bitcast_fusion) | copy-start | bytes 3145732
  41.8 2.1 %copy-start = (f32[8,32768]{1,0:T(8,128)S(1)}, f32[8,32768]{1,0:T(8,128)}, u32[]{:S(2)}) copy-start(f32[8,32768]{1,0:T(8,128)} %reshape.50) | copy-start | bytes 3145732
  61.0 12.4 %copy-start.2 = (bf16[1024,128]{1,0:T(8,128)(2,1)S(1)}, bf16[1024,128]{1,0:T(8,128)(2,1)}, u32[]{:S(2)}) copy-start(bf16[1024,128]{1,0:T(8,128)(2,1)} %param.7) | copy-start | bytes 786436
  61.1 12.4 %copy-start.3 = (bf16[1024,128]{1,0:T(8,128)(2,1)S(1)}, bf16[1024,128]{1,0:T(8,128)(2,1)}, u32[]{:S(2)}) copy-start(bf16[1024,128]{1,0:T(8,128)(2,1)} %param.12) | copy-start | bytes 786436
  61.1 12.4 %copy-start.4 = (f32[1024]{0:T(1024)S(1)}, f32[1024]{0:T(1024)}, u32[]{:S(2)}) copy-start(f32[1024]{0:T(1024)} %param.11) | copy-start | bytes 12292
  61.1 24.6 %copy-start.5 = (f32[1024]{0:T(1024)S(1)}, f32[1024]{0:T(1024)}, u32[]{:S(2)}) copy-start(f32[1024]{0:T(1024)} %param.13) | copy-start | bytes 12292
where the time goes:
time: 87.1 us; the launch traced here: 86.7 us
  blocking collectives  36.1 us (41%)
  matrix products  30.6 us (35%)
  local copies, waits for them, and re-layouts  8.56 us (10%)
  waiting for transfers between devices  4.67 us (5%)
  starting transfers between devices  3.41 us (4%)
  other arithmetic  2.43 us (3%)
    dot_general x18, matrix products, product(): jnp.dot(left, right, precision=HIGHEST, preferred_element_type=jnp.float32)  30.6 us
    all_to_all x1, blocking collectives, on_device(): lax.all_to_all(whole_out, 'seq', split_axis=1, concat_axis=0, tiled=True)  12.3 us
    psum x1, blocking collectives, on_device(): squares = lax.psum(jnp.sum(total * total, axis=0), 'ch')  12 us
    all_to_all x1, blocking collectives, on_device(): lax.all_to_all(product_in, 'seq', split_axis=0, concat_axis=1, tiled=True)  11.9 us
    all_to_all x1, waiting for transfers between devices, on_device(): lax.all_to_all(long_filter, 'seq', split_axis=0, concat_axis=1, tiled=True)  4.67 us
    all_to_all x1, starting transfers between devices, on_device(): lax.all_to_all(long_filter, 'seq', split_axis=0, concat_axis=1, tiled=True)  3.41 us
    neg x1, local copies, waits for them, and re-layouts, block_spectrum(): return (product(signal, cosine), -product(signal, sine))  2.63 us
  transfers between devices with their start and end apart: 1, of which 1 were waited for; matrix products, arithmetic and copies ran while one was open for 2% of the time, Pallas kernels for 0%

commit v1 on v0

--- a/solution.py
+++ b/solution.py
@@ -6,6 +6,12 @@
 
 D = 4096
 HIGHEST = lax.Precision.HIGHEST
+
+
+def unite_the_stacks_all(a_name, u):
+    return jnp.concatenate(
+        lax.all_to_all(jnp.stack(jnp.split(u, lax.axis_size(a_name), axis=0)), a_name, 0, 0), axis=1
+    )
 
 
 def tables(count, span, period):
@@ -60,7 +66,7 @@
     signal_f = product_in.astype(jnp.float32)
     whole_in, whole_filter = (
         lax.all_to_all(product_in, "seq", split_axis=0, concat_axis=1, tiled=True),
-        lax.all_to_all(long_filter, "seq", split_axis=0, concat_axis=1, tiled=True),
+        unite_the_stacks_all("seq", long_filter),
     )
     group = whole_in.shape[0]
 

time: 87.1 us -> 101 us (1.16); the launches traced: 86.7 us -> 99.4 us
  blocking collectives: 36.1 us -> 24.2 us
  matrix products: 30.6 us -> 40.1 us
  local copies, waits for them, and re-layouts: 8.56 us -> 16.1 us
  starting transfers between devices: 3.41 us -> 9.4 us
  other arithmetic: 2.43 us -> 4.1 us
    all_to_all x1 -> x0, blocking collectives: 11.9 us -> none  [on_device(): lax.all_to_all(product_in, 'seq', split_axis=0, concat_axis=1, tiled=True)]
    unnamed x12 -> x25, local copies, waits for them, and re-layouts: 0.03 us -> 9.94 us
    dot_general x18, matrix products: 30.6 us -> 40.1 us  [product(): jnp.dot(left, right, precision=HIGHEST, preferred_element_type=jnp.float32)]
    all_to_all x1 -> x2, starting transfers between devices: 3.41 us -> 9.4 us  [the longest x1 5.2 us: on_device(): lax.all_to_all(product_in, 'seq', split_axis=0, concat_axis=1, tiled=True)]
    neg x1 -> x0, local copies, waits for them, and re-layouts: 2.63 us -> none  [block_spectrum(): return (product(signal, cosine), -product(signal, sine))]
    another operation x0 -> x1, local copies, waits for them, and re-layouts: none -> 1.37 us  [unite_the_stacks_all(): jnp.stack(jnp.split(u, lax.axis_size(a_name), axis=0))]
    dot_general x1 -> x0, local copies, waits for them, and re-layouts: 1.36 us -> none  [product(): jnp.dot(left, right, precision=HIGHEST, preferred_element_type=jnp.float32)]
    reshape x1, local copies, waits for them, and re-layouts: 1.42 us -> 0.19 us  [on_device(): kernel_imag.reshape(blocks, -1)]
  transfers between devices with their start and end apart: 1 -> 2, of which waited for: 1 -> 1; matrix products, arithmetic and copies ran while one was open for 2% -> 13% of each run, Pallas kernels for 0% -> 0%
where the time goes in v1:
time: 101 us; the launch traced here: 99.4 us
  matrix products  40.1 us (40%)
  blocking collectives  24.2 us (24%)
  local copies, waits for them, and re-layouts  16.1 us (16%)
  starting transfers between devices  9.4 us (9%)
  waiting for transfers between devices  4.74 us (5%)
  other arithmetic  4.1 us (4%)
    dot_general x18, matrix products, product(): jnp.dot(left, right, precision=HIGHEST, preferred_element_type=jnp.float32)  40.1 us
    all_to_all x1, blocking collectives, on_device(): lax.all_to_all(whole_out, 'seq', split_axis=1, concat_axis=0, tiled=True)  12.3 us
    psum x1, blocking collectives, on_device(): squares = lax.psum(jnp.sum(total * total, axis=0), 'ch')  12 us
    unnamed x25, local copies, waits for them, and re-layouts  9.94 us
    all_to_all x1, starting transfers between devices, on_device(): lax.all_to_all(product_in, 'seq', split_axis=0, concat_axis=1, tiled=True)  5.2 us
    all_to_all x1, waiting for transfers between devices, unite_the_stacks_all(): lax.all_to_all(jnp.stack(jnp.split(u, lax.axis_size(a_name), axis=0)), a_...  4.74 us
    all_to_all x1, starting transfers between devices, unite_the_stacks_all(): lax.all_to_all(jnp.stack(jnp.split(u, lax.axis_size(a_name), axis=0)), a_...  4.2 us
  transfers between devices with their start and end apart: 2, of which 1 were waited for; matrix products, arithmetic and copies ran while one was open for 13% of the time, Pallas kernels for 0%

profile of v1, /device:TPU:0, one launch (start us, length us, event | category | flops | bytes accessed | tf_op | source)
XLA Modules:
  0.0 99.4 jit_solution(5487335403993297737)
XLA Ops:
  0.6 1.8 %multiply_convert_fusion.1 = bf16[1024,128]{1,0:T(8,128)(2,1)} fusion(bf16[1024,128]{1,0:T(8,128)(2,1)} %param.9, bf16[1024,128]{1,0:T(8,128)(2,1)} %param.8), kind=kLoop, calls=%fused_computation.21 | loop fusion | flops 524288 | bytes 786432 | tf_op jit(solution)/shard_map/convert_element_type | solution.py:63
  2.4 5.2 %all-to-all-start = ((bf16[8,128,128]{2,1,0:T(8,128)(2,1)}), bf16[8,128,128]{2,1,0:T(8,128)(2,1)S(1)}, u32[]{:S(2)}, u32[]{:S(2)}) async-start(bf16[8,128,128]{2,1,0:T(8,128)(2,1)} %bitcast), calls=%async_computation | async-start | bytes 524288 | tf_op jit(solution)/shard_map/all_to_all | solution.py:68
  18.6 4.2 %all-to-all-start.1 = ((bf16[8,128,128]{2,1,0:T(8,128)(2,1)}), bf16[8,128,128]{2,1,0:T(8,128)(2,1)S(1)}, u32[]{:S(2)}, u32[]{:S(2)}) async-start(bf16[8,128,128]{2,1,0:T(8,128)(2,1)} %bitcast_dynamic-update-slice_fusion), calls=%async_computation.1 | async-start | bytes 524288 | tf_op jit(solution)/shard_map/all_to_all | solution.py:13
  25.0 4.7 %all-to-all-done.1 = bf16[8,128,128]{2,1,0:T(8,128)(2,1)S(1)} async-done(((bf16[8,128,128]{2,1,0:T(8,128)(2,1)}), bf16[8,128,128]{2,1,0:T(8,128)(2,1)S(1)}, u32[]{:S(2)}, u32[]{:S(2)}) %all-to-all-start.1) | async-done | bytes 262176 | tf_op jit(solution)/shard_map/all_to_all | solution.py:13
  29.7 2.0 %convolution_negate_fusion = f32[1024,256]{1,0:T(8,128)} fusion(bf16[1024,128]{1,0:T(8,128)(2,1)S(1)} %bitcast.53), kind=kOutput, calls=%fused_computation.10 | convolution fusion | flops 403374080 | bytes 1310720 | tf_op jit(solution)/shard_map/dot_general | solution.py:25
  31.8 2.1 %fusion.25 = f32[1024,256]{1,0:T(8,128)} fusion(bf16[1024,128]{1,0:T(8,128)(2,1)S(1)} %bitcast.54), kind=kOutput, calls=%fused_computation.45 | convolution fusion | flops 403111936 | bytes 1310720 | tf_op jit(solution)/shard_map/dot_general | solution.py:25
  34.0 3.1 %fusion.48 = f32[16,32768]{1,0:T(8,128)} fusion(f32[8,32768]{1,0:T(8,128)S(1)} %reshape.49), kind=kOutput, calls=%fused_computation.75 | convolution fusion | flops 50333440 | bytes 3145728 | tf_op jit(solution)/shard_map/dot_general | solution.py:25
  37.4 3.2 %fusion.44 = f32[16,32768]{1,0:T(8,128)} fusion(f32[8,32768]{1,0:T(8,128)S(1)} %reshape.50), kind=kOutput, calls=%fused_computation.73 | convolution fusion | flops 50333440 | bytes 3145728 | tf_op jit(solution)/shard_map/dot_general | solution.py:25
  40.6 3.2 %convolution_add_fusion.1 = f32[16,32768]{1,0:T(8,128)} fusion(f32[16,32768]{1,0:T(8,128)S(1)} %copy-done, f32[8,32768]{1,0:T(8,128)S(1)} %reshape.50), kind=kOutput, calls=%fused_computation.3 | convolution fusion | flops 50857728 | bytes 5242880 | tf_op jit(solution)/shard_map/dot_general | solution.py:25
  43.9 3.2 %fusion.42 = f32[16,32768]{1,0:T(8,128)} fusion(f32[8,32768]{1,0:T(8,128)S(1)} %reshape.53), kind=kOutput, calls=%fused_computation.72 | convolution fusion | flops 50333440 | bytes 3145728 | tf_op jit(solution)/shard_map/dot_general | solution.py:25
  47.1 1.4 %reshape.52 = f32[8,32768]{1,0:T(8,128)S(1)} reshape(f32[1024,256]{1,0:T(8,128)} %fusion.25) | data formatting | bytes 2097152 | tf_op jit(solution)/shard_map/reshape | solution.py:86
  48.5 2.0 %fusion.46 = f32[16,32768]{1,0:T(8,128)S(1)} fusion(f32[8,32768]{1,0:T(8,128)S(1)} %reshape.52), kind=kOutput, calls=%fused_computation.74 | convolution fusion | flops 50333440 | bytes 3145728 | tf_op jit(solution)/shard_map/dot_general | solution.py:25
  50.5 1.9 %convolution_subtract_fusion = f32[16,32768]{1,0:T(8,128)S(1)} fusion(f32[16,32768]{1,0:T(8,128)S(1)} %copy-done.1, f32[8,32768]{1,0:T(8,128)S(1)} %reshape.52), kind=kOutput, calls=%fused_computation | convolution fusion | flops 50857728 | bytes 5242880 | tf_op jit(solution)/shard_map/dot_general | solution.py:25
  52.5 1.9 %convolution_add_fusion = f32[16,32768]{1,0:T(8,128)S(1)} fusion(f32[16,32768]{1,0:T(8,128)S(1)} %fusion.46, f32[8,32768]{1,0:T(8,128)S(1)} %reshape.53), kind=kOutput, calls=%fused_computation.2 | convolution fusion | flops 50857728 | bytes 5242880 | tf_op jit(solution)/shard_map/dot_general | solution.py:25
  54.7 2.5 %multiply_add_fusion = (f32[16,32768]{1,0:T(8,128)S(1)}, f32[16,32768]{1,0:T(8,128)S(1)}) fusion(f32[16,32768]{1,0:T(8,128)S(1)} %convolution_add_fusion, f32[16,32768]{1,0:T(8,128)S(1)} %copy-done.3, f32[16,32768]{1,0:T(8,128)S(1)} %convolution_subtract_fusion, f32[16,32768]{1,0:T(8,128)S(1)} %copy-done.2, f32[8,32768]{1,0:T(8,128)S(1)} %reshape.49), kind=kOutput, calls=%fused_computation.8 | convolution fusion | flops 54003456 | bytes 13631488 | tf_op jit(solution)/shard_map/dot_general | solution.py:25
  58.3 2.1 %fusion.61 = f32[8,32768]{1,0:T(8,128)} fusion(f32[16,32768]{1,0:T(8,128)S(1)} %get-tuple-element.5), kind=kOutput, calls=%fused_computation.82 | convolution fusion | flops 50333440 | bytes 3145728 | tf_op jit(solution)/shard_map/dot_general | solution.py:25
  60.4 2.2 %fusion = f32[8,32768]{1,0:T(8,128)} fusion(f32[8,32768]{1,0:T(8,128)S(1)} %fusion.59, f32[16,32768]{1,0:T(8,128)S(1)} %get-tuple-element.5), kind=kOutput, calls=%fused_computation.5 | convolution fusion | flops 50857728 | bytes 4194304 | tf_op jit(solution)/shard_map/dot_general | solution.py:25
  62.5 1.4 %reshape.55 = f32[1024,256]{1,0:T(8,128)S(1)} reshape(f32[8,32768]{1,0:T(8,128)} %fusion) | data formatting | bytes 2097152 | tf_op jit(solution)/shard_map/reshape | solution.py:91
  63.9 3.3 %fusion.1 = f32[8,32768]{1,0:T(8,128)} fusion(f32[8,32768]{1,0:T(8,128)} %fusion.61, f32[16,32768]{1,0:T(8,128)S(1)} %get-tuple-element.4), kind=kOutput, calls=%fused_computation.7 | convolution fusion | flops 50857728 | bytes 4194304 | tf_op jit(solution)/shard_map/dot_general | solution.py:25
  67.3 1.4 %reshape.54 = f32[1024,256]{1,0:T(8,128)S(1)} reshape(f32[8,32768]{1,0:T(8,128)} %fusion.1) | data formatting | bytes 2097152 | tf_op jit(solution)/shard_map/reshape | solution.py:90
  68.7 2.2 %fusion.10 = f32[1024,256]{1,0:T(8,128)S(1)} fusion(f32[1024,256]{1,0:T(8,128)S(1)} %reshape.54), kind=kOutput, calls=%fused_computation.29 | convolution fusion | flops 806223872 | bytes 2097152 | tf_op jit(solution)/shard_map/dot_general | solution.py:25
  70.8 2.0 %fusion.2 = f32[1024,256]{1,0:T(8,128)S(1)} fusion(f32[1024,256]{1,0:T(8,128)S(1)} %fusion.10, f32[1024,256]{1,0:T(8,128)S(1)} %reshape.55), kind=kOutput, calls=%fused_computation.13 | convolution fusion | flops 806748160 | bytes 3145728 | tf_op jit(solution)/shard_map/dot_general | solution.py:25
  73.0 12.3 %all_to_all.34 = f32[128,8,128]{2,0,1:T(8,128)S(1)} all-to-all(f32[128,8,128]{2,0,1:T(8,128)S(1)} %fusion.3), channel_id=1, replica_groups=mesh['seq'=8,'ch'=4] {'seq'}, dimensions={1} | all-to-all | bytes 1048576 | tf_op jit(solution)/shard_map/all_to_all | solution.py:96
  86.5 12.0 %psum.7 = f32[128]{0:T(128)S(1)} all-reduce(f32[128]{0:T(128)S(1)} %get-tuple-element.2), channel_id=1, replica_groups=mesh['seq'=8,'ch'=4] {'ch'}, use_global_device_ids=true, to_apply=%region_1.2 | all-reduce | flops 128 | bytes 1024 | tf_op jit(solution)/shard_map/psum | solution.py:100
  (38 shorter events, 17.5 us)
Async XLA Ops:
  2.4 16.2 %all-to-all-start = ((bf16[8,128,128]{2,1,0:T(8,128)(2,1)}), bf16[8,128,128]{2,1,0:T(8,128)(2,1)S(1)}, u32[]{:S(2)}, u32[]{:S(2)}) async-start(bf16[8,128,128]{2,1,0:T(8,128)(2,1)} %bitcast), calls=%async_computation | async-start | bytes 524288 | tf_op jit(solution)/shard_map/all_to_all | solution.py:68
  18.6 11.1 %all-to-all-start.1 = ((bf16[8,128,128]{2,1,0:T(8,128)(2,1)}), bf16[8,128,128]{2,1,0:T(8,128)(2,1)S(1)}, u32[]{:S(2)}, u32[]{:S(2)}) async-start(bf16[8,128,128]{2,1,0:T(8,128)(2,1)} %bitcast_dynamic-update-slice_fusion), calls=%async_computation.1 | async-start | bytes 524288 | tf_op jit(solution)/shard_map/all_to_all | solution.py:13
  37.4 3.2 %copy-start = (f32[16,32768]{1,0:T(8,128)S(1)}, f32[16,32768]{1,0:T(8,128)}, u32[]{:S(2)}) copy-start(f32[16,32768]{1,0:T(8,128)} %fusion.48) | copy-start | bytes 6291460
  40.6 3.2 %copy-start.4 = (f32[1024,256]{1,0:T(8,128)S(1)}, f32[1024,256]{1,0:T(8,128)}, u32[]{:S(2)}) copy-start(f32[1024,256]{1,0:T(8,128)} %convolution_negate_fusion) | copy-start | bytes 3145732
  48.5 2.0 %copy-start.1 = (f32[16,32768]{1,0:T(8,128)S(1)}, f32[16,32768]{1,0:T(8,128)}, u32[]{:S(2)}) copy-start(f32[16,32768]{1,0:T(8,128)} %fusion.42) | copy-start | bytes 6291460
  52.4 1.9 %copy-start.2 = (f32[16,32768]{1,0:T(8,128)S(1)}, f32[16,32768]{1,0:T(8,128)}, u32[]{:S(2)}) copy-start(f32[16,32768]{1,0:T(8,128)} %fusion.44) | copy-start | bytes 6291460
  52.5 2.2 %copy-start.3 = (f32[16,32768]{1,0:T(8,128)S(1)}, f32[16,32768]{1,0:T(8,128)}, u32[]{:S(2)}) copy-start(f32[16,32768]{1,0:T(8,128)} %convolution_add_fusion.1) | copy-start | bytes 6291460
  72.8 12.4 %copy-start.5 = (bf16[1024,128]{1,0:T(8,128)(2,1)S(1)}, bf16[1024,128]{1,0:T(8,128)(2,1)}, u32[]{:S(2)}) copy-start(bf16[1024,128]{1,0:T(8,128)(2,1)} %param.7) | copy-start | bytes 786436
  72.8 12.4 %copy-start.6 = (bf16[1024,128]{1,0:T(8,128)(2,1)S(1)}, bf16[1024,128]{1,0:T(8,128)(2,1)}, u32[]{:S(2)}) copy-start(bf16[1024,128]{1,0:T(8,128)(2,1)} %param.12) | copy-start | bytes 786436
  72.8 12.4 %copy-start.7 = (f32[1024]{0:T(1024)S(1)}, f32[1024]{0:T(1024)}, u32[]{:S(2)}) copy-start(f32[1024]{0:T(1024)} %param.11) | copy-start | bytes 12292
  72.9 25.6 %copy-start.8 = (f32[1024]{0:T(1024)S(1)}, f32[1024]{0:T(1024)}, u32[]{:S(2)}) copy-start(f32[1024]{0:T(1024)} %param.13) | copy-start | bytes 12292
